TPU v7x, 32 devices: a whole 2x2x4 slice. The times are simulated.
32 devices in a mesh: section: 1, expert: 8 (over z, y), dp: 4 (over x, core).
Axes of the slice: x: 2, y: 2, z: 4, core: 2. Of those that a mesh axis runs over, the one named last changes fastest.
Arguments:
- fwd_resid: bfloat16 [1, 1024, 2048], P('section', 'expert', 'dp'), may hold values from -6 to 6
- fwd_normed: bfloat16 [1, 1024, 2048], P('section', 'expert', 'dp'), may hold values from -6 to 6
- fwd_routes: int32 [1, 1024, 8], P('section', 'expert'), may hold values from 0 to 15, all different within a row; in each aligned block of 128 rows (0 to 127, 128 to 255, ..., all dimensions but the last counted through in order) at most 65 rows name the same one
- fwd_probs: float32 [1, 1024, 8], P('section', 'expert'), may hold values from 0.02 to 0.3
- bwd_grad: bfloat16 [1, 1024, 2048], P('section', 'expert', 'dp'), may hold values from -6 to 6
- bwd_routes: int32 [1, 1024, 8], P('section', 'expert'), may hold values from 0 to 15, all different within a row; in each aligned block of 128 rows (0 to 127, 128 to 255, ..., all dimensions but the last counted through in order) at most 65 rows name the same one
- bwd_probs: float32 [1, 1024, 8], P('section', 'expert'), may hold values from 0.02 to 0.3
- saved_gate: bfloat16 [1, 32, 520, 192], P('section', ('expert', 'dp')), may hold values from -6 to 6
- saved_up: bfloat16 [1, 32, 520, 192], P('section', ('expert', 'dp')), may hold values from -6 to 6
- w_gate: bfloat16 [1, 32, 2048, 192], P('section', ('expert', 'dp')), may hold values from -0.125 to 0.125
- w_up: bfloat16 [1, 32, 2048, 192], P('section', ('expert', 'dp')), may hold values from -0.125 to 0.125
- w_down: bfloat16 [1, 32, 192, 2048], P('section', ('expert', 'dp')), may hold values from -0.3125 to 0.3125
Outputs:
- fwd_next: bfloat16 [1, 1024, 2048], P('section', 'expert', 'dp')
- bwd_next: bfloat16 [1, 1024, 2048], P('section', 'expert', 'dp')
Inputs may be any that keep to these rules, and one draw needn't show every extreme that they name: `fwd_routes`: each token names 8 different experts. Within the tokens of one device (aligned blocks of 128 tokens of one section) no expert is named more than 65 times, a bound that some block reaches. `bwd_routes`: each token names 8 different experts. Within the tokens of one device (aligned blocks of 128 tokens of one section) no expert is named more than 65 times, a bound that some block reaches.
All inputs are finite; a program needn't handle non-finite values.
Results may differ from a plain program's by a relative error of at most 0.0065.
Values may be sent and summed in bfloat16 or wider, within the bound.
A program may use at most 64 MiB of HBM per device.

v0:
```python
import functools

import jax
import jax.numpy as jnp
from jax import lax
from jax.experimental import pallas as pl
from jax.experimental.pallas import tpu as pltpu
from jax.sharding import PartitionSpec as P

F32 = jnp.float32
BF16 = jnp.bfloat16
MESH = pl.DeviceIdType.MESH


def round_up(value, unit):
    return -(-value // unit) * unit


def kernel(
    n, xs, top, cap,
    resid, normed, grad, rp, sg_hbm, su_hbm, wg_hbm, wu_hbm, wd_hbm,
    fwd_out, bwd_out,
    sg, su, wg, wu, wd, fac,
    meta_s, meta_z, meta_y, tok, rows, stag, keep, half_s, half_r, mixin, eo_s,
    yout, yin, zacc, zout, zin,
    load_sem, ms_sem, mr_sem, my_sem, zs_sem, zr_sem, ys_sem, yr_sem,
    xs_sem, xr_sem, cs_sem, cr_sem, hs_sem, hr_sem, es_sem, er_sem,
    ry_sem, rzs_sem, rzr_sem,
):
    half = n // 2
    tokens, width = normed.shape
    experts = n * xs
    chunk = rows.shape[-2]
    slots = sg_hbm.shape[0]
    e = lax.axis_index("expert")
    d = lax.axis_index("dp")
    hi, lo = lax.div(e, 2), lax.rem(e, 2)
    x, core = lax.div(d, 2), lax.rem(d, 2)

    def z_dev(k):
        return {"expert": lax.rem(hi + k, half) * 2 + lo, "dp": d}

    y_dev = {"expert": hi * 2 + 1 - lo, "dp": d}

    def x_dev(k):
        return {"expert": e, "dp": lax.rem(x + k, xs) * 2 + core}

    c_dev = {"expert": e, "dp": x * 2 + 1 - core}
    pending = []

    def send(src, dst, s_sem, r_sem, dev):
        copy = pltpu.make_async_remote_copy(
            src_ref=src, dst_ref=dst, send_sem=s_sem, recv_sem=r_sem,
            device_id=dev, device_id_type=MESH,
        )
        copy.start()
        pending.append(copy)

    def arrived(dst, s_sem, r_sem, dev):
        pltpu.make_async_remote_copy(
            src_ref=dst, dst_ref=dst, send_sem=s_sem, recv_sem=r_sem,
            device_id=dev, device_id_type=MESH,
        ).wait_recv()

    barrier = pltpu.get_barrier_semaphore()
    partners = [z_dev(k) for k in range(1, half)] + [y_dev]
    partners += [x_dev(k) for k in range(1, xs)] + [c_dev]
    for dev in partners:
        pl.semaphore_signal(barrier, inc=1, device_id=dev, device_id_type=MESH)

    loads = [
        pltpu.make_async_copy(a, b, load_sem.at[i])
        for i, (a, b) in enumerate(
            ((sg_hbm, sg), (su_hbm, su), (wg_hbm, wg), (wu_hbm, wu), (wd_hbm, wd))
        )
    ]
    for load in loads:
        load.start()

    expert_ids = lax.broadcasted_iota(jnp.int32, (experts, tokens), 0).astype(F32)
    tri = (
        lax.broadcasted_iota(jnp.int32, (tokens, tokens), 0)
        < lax.broadcasted_iota(jnp.int32, (tokens, tokens), 1)
    ).astype(F32).astype(BF16)
    for p in range(2):
        hits = jnp.zeros((experts, tokens), F32)
        weight = jnp.zeros((experts, tokens), F32)
        for j in range(top):
            same = rp[2 * p * top + j : 2 * p * top + j + 1, :] == expert_ids
            hits = hits + jnp.where(same, 1.0, 0.0)
            prob = rp[(2 * p + 1) * top + j : (2 * p + 1) * top + j + 1, :]
            weight = weight + jnp.where(same, prob, 0.0)
        before = jnp.dot(hits.astype(BF16), tri, preferred_element_type=F32)
        place = jnp.where(hits > 0.0, before, -1000000.0)
        for g in range(n):
            meta_s[g, 2 * p * xs : (2 * p + 1) * xs, :] = place[g * xs : (g + 1) * xs, :]
            meta_s[g, (2 * p + 1) * xs : (2 * p + 2) * xs, :] = weight[g * xs : (g + 1) * xs, :]
    meta_z[0, 0] = meta_s[e]
    meta_z[1, 0] = meta_s[hi * 2 + 1 - lo]

    pl.semaphore_wait(barrier, len(partners))

    for k in range(1, half):
        to = lax.rem(hi + k, half) * 2
        for c in range(2):
            send(
                meta_s.at[to + (lo if c == 0 else 1 - lo)], meta_z.at[c, half - k],
                ms_sem.at[c, k], mr_sem.at[c, half - k], z_dev(k),
            )
    sources = (normed, grad)
    for p in range(2):
        for k in range(1, half):
            send(sources[p], tok.at[p, 0, half - k], zs_sem.at[p, k], zr_sem.at[p, half - k], z_dev(k))
        send(sources[p], tok.at[p, 1, 0], ys_sem.at[p, 0], yr_sem.at[p, 0], y_dev)
        tok[p, 0, 0] = sources[p][...]

    def forward_y(p):
        for r in range(1, half):
            arrived(tok.at[p, 0, r], zs_sem.at[p, r], zr_sem.at[p, r], z_dev(r))
            send(tok.at[p, 0, r], tok.at[p, 1, r], ys_sem.at[p, r], yr_sem.at[p, r], y_dev)

    def meta_row(c, r, row):
        if c == 0:
            return meta_z[0, r, pl.ds(row, 1), :]
        return meta_y[r, pl.ds(row, 1), :]

    def pack(p, c):
        if c == 1:
            for r in range(half):
                arrived(tok.at[p, 1, r], ys_sem.at[p, r], yr_sem.at[p, r], y_dev)
        slot_ids = lax.broadcasted_iota(jnp.int32, (chunk, tokens), 0).astype(F32)
        block = tok[p, c].reshape(half * tokens, width)
        for k in list(range(1, xs)) + [0]:
            line = 2 * p * xs + lax.rem(x + k, xs)
            parts = [
                jnp.where(slot_ids == meta_row(c, r, line) + float(r * cap), 1.0, 0.0).astype(BF16)
                for r in range(half)
            ]
            packed = jnp.dot(
                jnp.concatenate(parts, axis=1), block, preferred_element_type=F32
            ).astype(BF16)
            if k == 0:
                rows[p, c, 0, 0] = packed
                send(rows.at[p, c, 0, 0], rows.at[p, c, 0, 1], cs_sem.at[p, c, 0], cr_sem.at[p, c, 0], c_dev)
            else:
                stag[p, c, k] = packed
                send(stag.at[p, c, k], rows.at[p, c, xs - k, 0], xs_sem.at[p, c, k], xr_sem.at[p, c, xs - k], x_dev(k))

    def forward_core(p, c):
        for r in range(1, xs):
            arrived(rows.at[p, c, r, 0], xs_sem.at[p, c, r], xr_sem.at[p, c, r], x_dev(r))
            send(rows.at[p, c, r, 0], rows.at[p, c, r, 1], cs_sem.at[p, c, r], cr_sem.at[p, c, r], c_dev)

    def feature(r, other):
        at = lax.rem(x + r, xs) * 2 + (1 - core if other else core)
        return pl.ds(pl.multiple_of(at * width, width), width)

    nt = (((1,), (1,)), ((), ()))

    def compute(p, c):
        parts = [(r, o) for r in range(xs) for o in range(2)]
        first, second = None, None
        for r, o in parts:
            if o == 1:
                arrived(rows.at[p, c, r, 1], cs_sem.at[p, c, r], cr_sem.at[p, c, r], c_dev)
            piece = rows[p, c, r, o]
            if p == 0:
                a = jnp.dot(piece, wg[feature(r, o), :], preferred_element_type=F32)
                b = jnp.dot(piece, wu[feature(r, o), :], preferred_element_type=F32)
                first = a if first is None else first + a
                second = b if second is None else second + b
            else:
                a = lax.dot_general(piece, wd[:, feature(r, o)], nt, preferred_element_type=F32)
                first = a if first is None else first + a
        if p == 0:
            hidden = (jax.nn.silu(first) * second).astype(BF16)
        else:
            grad_gate = (first * fac[0, c]).astype(BF16)
            grad_up = (first * fac[1, c]).astype(BF16)
        for o in (1, 0):
            for r in range(xs):
                if p == 0:
                    res = jnp.dot(hidden, wd[:, feature(r, o)], preferred_element_type=F32)
                else:
                    res = lax.dot_general(grad_gate, wg[feature(r, o), :], nt, preferred_element_type=F32)
                    res = res + lax.dot_general(grad_up, wu[feature(r, o), :], nt, preferred_element_type=F32)
                if o == 1:
                    half_s[p, c, r] = res.astype(BF16)
                    send(half_s.at[p, c, r], half_r.at[p, c, r], hs_sem.at[p, c, r], hr_sem.at[p, c, r], c_dev)
                else:
                    keep[p, c, r] = res.astype(BF16)

    def join(p, c):
        for r in list(range(1, xs)) + [0]:
            arrived(half_r.at[p, c, r], hs_sem.at[p, c, r], hr_sem.at[p, c, r], c_dev)
            total = (keep[p, c, r].astype(F32) + half_r[p, c, r].astype(F32)).astype(BF16)
            if r == 0:
                mixin[p, c, 0] = total
            else:
                eo_s[p, c, r] = total
                send(eo_s.at[p, c, r], mixin.at[p, c, xs - r], es_sem.at[p, c, r], er_sem.at[p, c, xs - r], x_dev(r))

    def mix(p, c):
        for r in range(1, xs):
            arrived(mixin.at[p, c, r], es_sem.at[p, c, r], er_sem.at[p, c, r], x_dev(r))
        slot_ids = lax.broadcasted_iota(jnp.int32, (tokens, chunk), 1).astype(F32)
        pad = round_up(2 * xs, 8) - 2 * xs
        for r in range(half):
            lines = []
            for k in range(xs):
                at = lax.rem(x + k, xs)
                lines.append(meta_row(c, r, 2 * p * xs + at))
                lines.append(meta_row(c, r, (2 * p + 1) * xs + at))
            if pad:
                lines.append(jnp.zeros((pad, tokens), F32))
            cols = jnp.concatenate(lines, axis=0).T
            mats = [
                jnp.where(
                    slot_ids == cols[:, 2 * k : 2 * k + 1] + float(r * cap),
                    cols[:, 2 * k + 1 : 2 * k + 2], 0.0,
                ).astype(BF16)
                for k in range(xs)
            ]
            out = jnp.zeros((tokens, width), F32)
            for k in range(xs):
                out = out + jnp.dot(mats[k], mixin[p, c, k], preferred_element_type=F32)
            if c == 1:
                yout[p, r] = out.astype(BF16)
                send(yout.at[p, r], yin.at[p, r], ry_sem.at[0, p, r], ry_sem.at[1, p, r], y_dev)
            else:
                zacc[p, r] = out

    def scatter_z(p):
        for r in list(range(1, half)) + [0]:
            arrived(yin.at[p, r], ry_sem.at[0, p, r], ry_sem.at[1, p, r], y_dev)
            total = zacc[p, r] + yin[p, r].astype(F32)
            if r == 0:
                zacc[p, 0] = total
            else:
                zout[p, r] = total.astype(BF16)
                send(zout.at[p, r], zin.at[p, half - r], rzs_sem.at[p, r], rzr_sem.at[p, half - r], z_dev(r))

    def finish(p):
        total = zacc[p, 0]
        if p == 0:
            total = total + resid[...].astype(F32)
        for r in range(1, half):
            arrived(zin.at[p, r], rzs_sem.at[p, r], rzr_sem.at[p, r], z_dev(r))
            total = total + zin[p, r].astype(F32)
        (fwd_out, bwd_out)[p][...] = total.astype(BF16)

    loads[0].wait()
    loads[1].wait()
    for c in range(2):
        at = lax.broadcasted_iota(jnp.int32, (chunk, slots), 0)
        turn = jnp.zeros((chunk, slots), jnp.int32)
        for k in range(1, half):
            turn = turn + jnp.where(at >= k * cap, 1, 0)
        place = at - turn * cap
        turn = turn + hi
        turn = jnp.where(turn >= half, turn - half, turn)
        origin = (turn * 2 + (lo if c == 0 else 1 - lo)) * cap + place
        hit = (origin == lax.broadcasted_iota(jnp.int32, (chunk, slots), 1)) & (at < half * cap)
        perm = jnp.where(hit, 1.0, 0.0).astype(BF16)
        gval = jnp.dot(perm, sg[...], preferred_element_type=F32)
        uval = jnp.dot(perm, su[...], preferred_element_type=F32)
        sig = jax.nn.sigmoid(gval)
        fac[0, c] = uval * sig * (1.0 + gval * (1.0 - sig))
        fac[1, c] = gval * sig

    for k in range(1, half):
        for c in range(2):
            arrived(meta_z.at[c, k], ms_sem.at[c, k], mr_sem.at[c, k], z_dev(k))
    send(meta_z.at[1], meta_y, my_sem.at[0], my_sem.at[1], y_dev)
    forward_y(0)
    pack(0, 0)
    forward_y(1)
    arrived(meta_y, my_sem.at[0], my_sem.at[1], y_dev)
    pack(0, 1)
    forward_core(0, 0)
    pack(1, 0)
    forward_core(0, 1)
    for load in loads[2:]:
        load.wait()
    compute(0, 1)
    pack(1, 1)
    join(0, 1)
    compute(0, 0)
    forward_core(1, 0)
    join(0, 0)
    forward_core(1, 1)
    mix(0, 1)
    compute(1, 1)
    join(1, 1)
    mix(0, 0)
    scatter_z(0)
    compute(1, 0)
    join(1, 0)
    mix(1, 1)
    mix(1, 0)
    finish(0)
    scatter_z(1)
    finish(1)
    for copy in pending:
        copy.wait_send()


def body(
    fwd_resid, fwd_normed, fwd_routes, fwd_probs, bwd_grad, bwd_routes, bwd_probs,
    saved_gate, saved_up, w_gate, w_up, w_down,
):
    n = lax.axis_size("expert")
    dp = lax.axis_size("dp")
    sections = lax.axis_size("section")
    xs = dp // 2
    half = n // 2
    tokens, width = fwd_normed.shape[1:]
    top = fwd_routes.shape[2]
    slots, hidden = saved_gate.shape[2:]
    feats = w_gate.shape[2]
    cap = slots // n
    chunk = round_up(half * cap, 16)
    meta_rows = 4 * xs
    rp = jnp.concatenate(
        [
            fwd_routes[0].astype(F32).T, fwd_probs[0].T,
            bwd_routes[0].astype(F32).T, bwd_probs[0].T,
        ],
        axis=0,
    )
    vmem = pl.BlockSpec(memory_space=pltpu.VMEM)
    hbm = pl.BlockSpec(memory_space=pl.ANY)
    dma = pltpu.SemaphoreType.DMA
    out = jax.ShapeDtypeStruct((tokens, width), BF16)
    fwd_out, bwd_out = pl.pallas_call(
        functools.partial(kernel, n, xs, top, cap),
        out_shape=(out, out),
        in_specs=[vmem] * 4 + [hbm] * 5,
        out_specs=(vmem, vmem),
        scratch_shapes=[
            pltpu.VMEM((slots, hidden), BF16),
            pltpu.VMEM((slots, hidden), BF16),
            pltpu.VMEM((feats, hidden), BF16),
            pltpu.VMEM((feats, hidden), BF16),
            pltpu.VMEM((hidden, feats), BF16),
            pltpu.VMEM((2, 2, chunk, hidden), F32),
            pltpu.VMEM((n, meta_rows, tokens), F32),
            pltpu.VMEM((2, half, meta_rows, tokens), F32),
            pltpu.VMEM((half, meta_rows, tokens), F32),
            pltpu.VMEM((2, 2, half, tokens, width), BF16),
            pltpu.VMEM((2, 2, xs, 2, chunk, width), BF16),
            pltpu.VMEM((2, 2, xs, chunk, width), BF16),
            pltpu.VMEM((2, 2, xs, chunk, width), BF16),
            pltpu.VMEM((2, 2, xs, chunk, width), BF16),
            pltpu.VMEM((2, 2, xs, chunk, width), BF16),
            pltpu.VMEM((2, 2, xs, chunk, width), BF16),
            pltpu.VMEM((2, 2, xs, chunk, width), BF16),
            pltpu.VMEM((2, half, tokens, width), BF16),
            pltpu.VMEM((2, half, tokens, width), BF16),
            pltpu.VMEM((2, half, tokens, width), F32),
            pltpu.VMEM((2, half, tokens, width), BF16),
            pltpu.VMEM((2, half, tokens, width), BF16),
            dma((5,)),
            dma((2, half)), dma((2, half)), dma((2,)),
            dma((2, half)), dma((2, half)), dma((2, half)), dma((2, half)),
            dma((2, 2, xs)), dma((2, 2, xs)), dma((2, 2, xs)), dma((2, 2, xs)),
            dma((2, 2, xs)), dma((2, 2, xs)), dma((2, 2, xs)), dma((2, 2, xs)),
            dma((2, 2, half)), dma((2, half)), dma((2, half)),
        ],
        compiler_params=pltpu.CompilerParams(
            collective_id=0, has_side_effects=True, vmem_limit_bytes=60 * 1024 * 1024
        ),
    )(
        fwd_resid[0], fwd_normed[0], bwd_grad[0], rp,
        saved_gate[0, 0], saved_up[0, 0], w_gate[0, 0], w_up[0, 0], w_down[0, 0],
    )
    fwd_next, bwd_next = fwd_out[None], bwd_out[None]
    if sections > 1:
        up = [(i, (i + 1) % sections) for i in range(sections)]
        fwd_next = lax.ppermute(fwd_next, "section", up)
        bwd_next = lax.ppermute(bwd_next, "section", [(j, i) for i, j in up])
    return (fwd_next, bwd_next)


def solution(mesh):
    tok = P("section", "expert", "dp")
    route = P("section", "expert", None)
    unit = P("section", ("expert", "dp"), None, None)
    return jax.shard_map(
        body,
        mesh=mesh,
        in_specs=(tok, tok, route, route, tok, route, route, unit, unit, unit, unit, unit),
        out_specs=(tok, tok),
        check_vma=False,
    )
```

profile of v0, /device:TPU:0, one launch (start us, length us, event | category | flops | bytes accessed | tf_op | source)
XLA Modules:
  0.0 107.6 jit_solution(13945576180469588571)
XLA Ops:
  0.6 0.0 copy-start
  0.6 0.8 convert_bitcast_fusion
  1.4 1.3 %pad_maximum_fusion.rp = f32[32,128]{1,0:T(8,128)} fusion(f32[8,128]{1,0:T(8,128)} %bitcast.34, f32[8,128]{1,0:T(8,128)S(1)} %get-tuple-element.6, f32[8,128]{1,0:T(8,128)} %bitcast.35, f32[8,128]{1,0:T(8,128)S(1)} %get-tuple-element.7), kind=kLoop, calls=%fused_computation | loop fusion | flops 12288 | bytes 32768 | tf_op jit(solution)/shard_map/concatenate | solution.py:324
  2.7 1.8 %copy.14 = bf16[1,1,520,192]{3,2,1,0:T(8,128)(2,1)} copy(bf16[1,1,520,192]{2,3,1,0:T(8,128)(2,1)} %param.19) | data formatting | bytes 399360 | tf_op args[7]
  4.5 1.8 %copy.15 = bf16[1,1,520,192]{3,2,1,0:T(8,128)(2,1)} copy(bf16[1,1,520,192]{2,3,1,0:T(8,128)(2,1)} %param.20) | data formatting | bytes 399360 | tf_op args[8]
  6.3 0.0 copy-done
  6.3 0.0 copy-start.1
  6.3 1.3 %copy.16 = bf16[1,1,2048,192]{3,2,1,0:T(8,128)(2,1)} copy(bf16[1,1,2048,192]{2,3,1,0:T(8,128)(2,1)S(1)} %copy-done) | data formatting | bytes 1572864 | tf_op args[9]
  7.6 0.0 copy-done.1
  7.6 1.3 %copy.17 = bf16[1,1,2048,192]{3,2,1,0:T(8,128)(2,1)} copy(bf16[1,1,2048,192]{2,3,1,0:T(8,128)(2,1)S(1)} %copy-done.1) | data formatting | bytes 1572864 | tf_op args[10]
  8.9 96.4 %shard_map.131 = (bf16[128,512]{1,0:T(8,128)(2,1)}, bf16[128,512]{1,0:T(8,128)(2,1)}) custom-call(bf16[128,512]{1,0:T(8,128)(2,1)} %bitcast.31, bf16[128,512]{1,0:T(8,128)(2,1)} %bitcast.32, bf16[128,512]{1,0:T(8,128)(2,1)} %bitcast.33, f32[32,128]{1,0:T(8,128)} %pad_maximum_fusion.rp, bf16[520,192]{1,0:T(8,128)(2,1)} %bitcast.26, ...), custom_call_target="tpu_custom_call" | custom-call | tf_op jit(solution)/shard_map/pallas_call | solution.py:335
  105.3 0.0 copy-start.2
  105.3 1.6 %copy.20 = bf16[1,128,512]{2,1,0:T(8,128)(2,1)} copy(bf16[1,128,512]{2,1,0:T(8,128)(2,1)} %bitcast.30) | data formatting | bytes 262144
  106.9 0.0 copy-done.2
  106.9 0.7 copy.21
Async XLA Ops:
  0.6 5.7 %copy-start = (bf16[1,1,2048,192]{2,3,1,0:T(8,128)(2,1)S(1)}, bf16[1,1,2048,192]{2,3,1,0:T(8,128)(2,1)}, u32[]{:S(2)}) copy-start(bf16[1,1,2048,192]{2,3,1,0:T(8,128)(2,1)} %param.21) | copy-start | bytes 2359300
  6.3 1.3 %copy-start.1 = (bf16[1,1,2048,192]{2,3,1,0:T(8,128)(2,1)S(1)}, bf16[1,1,2048,192]{2,3,1,0:T(8,128)(2,1)}, u32[]{:S(2)}) copy-start(bf16[1,1,2048,192]{2,3,1,0:T(8,128)(2,1)} %param.22) | copy-start | bytes 2359300
  105.3 1.6 %copy-start.2 = (bf16[128,512]{1,0:T(8,128)(2,1)S(1)}, bf16[128,512]{1,0:T(8,128)(2,1)}, u32[]{:S(2)}) copy-start(bf16[128,512]{1,0:T(8,128)(2,1)} %get-tuple-element.5) | copy-start | bytes 393220
where the time goes:
time: 108 us
  Pallas kernels  96.4 us (89%)
  local copies, waits for them, and re-layouts  8.42 us (8%)
  other arithmetic  2.09 us (2%)
    pallas_call x1, Pallas kernels, body(): pl.pallas_call(functools.partial(kernel, n, xs, top, cap), out_shape=(out...  96.4 us
    unnamed x12, local copies, waits for them, and re-layouts  8.42 us

commit v1 on v0

v1 whole, which is shorter than its diff:
```python
import functools

import jax
import jax.numpy as jnp
from jax import lax
from jax.experimental import pallas as pl
from jax.experimental.pallas import tpu as pltpu
from jax.sharding import PartitionSpec as P

F32 = jnp.float32
BF16 = jnp.bfloat16
MESH = pl.DeviceIdType.MESH


def round_up(value, unit):
    return -(-value // unit) * unit


def kernel(
    n, xs, top, cap,
    normed, grad, fr, fp, br, bp, sg_hbm, su_hbm, wg_hbm, wu_hbm, wd_hbm,
    fwd_out, bwd_out,
    sg, su, wg, wu, wd, fac,
    meta_s, meta_z, meta_y, tok, rows, stag, keep, half_s, half_r, mixin, eo_s,
    yout, yin, zacc, zout, zin,
    load_sem, ms_sem, mr_sem, my_sem, zs_sem, zr_sem, ys_sem, yr_sem,
    xs_sem, xr_sem, cs_sem, cr_sem, hs_sem, hr_sem, es_sem, er_sem,
    ry_sem, rzs_sem, rzr_sem,
):
    half = n // 2
    tokens, width = normed.shape
    experts = n * xs
    chunk = rows.shape[-2]
    slots = sg_hbm.shape[1]
    e = lax.axis_index("expert")
    d = lax.axis_index("dp")
    hi, lo = lax.div(e, 2), lax.rem(e, 2)
    x, core = lax.div(d, 2), lax.rem(d, 2)

    def z_dev(k):
        return {"expert": lax.rem(hi + k, half) * 2 + lo, "dp": d}

    y_dev = {"expert": hi * 2 + 1 - lo, "dp": d}

    def x_dev(k):
        return {"expert": e, "dp": lax.rem(x + k, xs) * 2 + core}

    c_dev = {"expert": e, "dp": x * 2 + 1 - core}
    pending = []

    def send(src, dst, s_sem, r_sem, dev):
        copy = pltpu.make_async_remote_copy(
            src_ref=src, dst_ref=dst, send_sem=s_sem, recv_sem=r_sem,
            device_id=dev, device_id_type=MESH,
        )
        copy.start()
        pending.append(copy)

    def arrived(dst, s_sem, r_sem, dev):
        pltpu.make_async_remote_copy(
            src_ref=dst, dst_ref=dst, send_sem=s_sem, recv_sem=r_sem,
            device_id=dev, device_id_type=MESH,
        ).wait_recv()

    barrier = pltpu.get_barrier_semaphore()
    partners = [z_dev(k) for k in range(1, half)] + [y_dev]
    partners += [x_dev(k) for k in range(1, xs)] + [c_dev]
    for dev in partners:
        pl.semaphore_signal(barrier, inc=1, device_id=dev, device_id_type=MESH)

    loads = [
        pltpu.make_async_copy(a, b, load_sem.at[i])
        for i, (a, b) in enumerate(
            ((sg_hbm, sg), (su_hbm, su), (wg_hbm, wg), (wu_hbm, wu), (wd_hbm, wd))
        )
    ]
    for load in loads:
        load.start()

    expert_ids = lax.broadcasted_iota(jnp.int32, (experts, tokens), 0)
    tri = (
        lax.broadcasted_iota(jnp.int32, (tokens, tokens), 0)
        < lax.broadcasted_iota(jnp.int32, (tokens, tokens), 1)
    ).astype(F32).astype(BF16)
    for p, (routes, probs) in enumerate(((fr, fp), (br, bp))):
        hits = jnp.zeros((experts, tokens), F32)
        weight = jnp.zeros((experts, tokens), F32)
        for j in range(top):
            same = routes[j : j + 1, :] == expert_ids
            hits = hits + jnp.where(same, 1.0, 0.0)
            weight = weight + jnp.where(same, probs[j : j + 1, :], 0.0)
        before = jnp.dot(hits.astype(BF16), tri, preferred_element_type=F32)
        place = jnp.where(hits > 0.0, before, -1000000.0)
        for g in range(n):
            meta_s[g, 2 * p * xs : (2 * p + 1) * xs, :] = place[g * xs : (g + 1) * xs, :]
            meta_s[g, (2 * p + 1) * xs : (2 * p + 2) * xs, :] = weight[g * xs : (g + 1) * xs, :]
    meta_z[0, 0] = meta_s[e]
    sources = (normed, grad)
    for p in range(2):
        tok[p, 0, 0] = sources[p][...]

    pl.semaphore_wait(barrier, len(partners))

    send(meta_s.at[hi * 2 + 1 - lo], meta_y.at[0], my_sem.at[0, 0], my_sem.at[1, 0], y_dev)
    for k in range(1, half):
        to = lax.rem(hi + k, half) * 2
        for c in range(2):
            send(
                meta_s.at[to + (lo if c == 0 else 1 - lo)], meta_z.at[c, half - k],
                ms_sem.at[c, k], mr_sem.at[c, half - k], z_dev(k),
            )

    def start_y(p):
        send(sources[p], tok.at[p, 0, 1], ys_sem.at[p, 0], yr_sem.at[p, 0], y_dev)

    start_y(0)
    for p in range(2):
        for k in range(1, half):
            send(sources[p], tok.at[p, half - k, 0], zs_sem.at[p, k], zr_sem.at[p, half - k], z_dev(k))

    def forward_y(p, r):
        if r == 0:
            if p == 1:
                start_y(1)
            return
        if p == 0:
            for c in range(2):
                arrived(meta_z.at[c, r], ms_sem.at[c, r], mr_sem.at[c, r], z_dev(r))
            send(meta_z.at[1, r], meta_y.at[r], my_sem.at[0, r], my_sem.at[1, r], y_dev)
        arrived(tok.at[p, r, 0], zs_sem.at[p, r], zr_sem.at[p, r], z_dev(r))
        send(tok.at[p, r, 0], tok.at[p, r, 1], ys_sem.at[p, r], yr_sem.at[p, r], y_dev)

    def meta_row(c, r, row):
        if c == 0:
            return meta_z[0, r, pl.ds(row, 1), :]
        return meta_y[r, pl.ds(row, 1), :]

    def pack(p, r):
        if p == 0:
            arrived(meta_y.at[r], my_sem.at[0, r], my_sem.at[1, r], y_dev)
        arrived(tok.at[p, r, 1], ys_sem.at[p, r], yr_sem.at[p, r], y_dev)
        slot_ids = lax.broadcasted_iota(jnp.int32, (chunk, tokens), 0).astype(F32)
        block = tok[p, r].reshape(2 * tokens, width)
        for k in list(range(1, xs)) + [0]:
            line = 2 * p * xs + lax.rem(x + k, xs)
            parts = [
                jnp.where(slot_ids == meta_row(c, r, line) + float(c * cap), 1.0, 0.0).astype(BF16)
                for c in range(2)
            ]
            packed = jnp.dot(
                jnp.concatenate(parts, axis=1), block, preferred_element_type=F32
            ).astype(BF16)
            if k == 0:
                rows[p, r, 0, 0] = packed
                send(rows.at[p, r, 0, 0], rows.at[p, r, 0, 1], cs_sem.at[p, r, 0], cr_sem.at[p, r, 0], c_dev)
            else:
                stag[p, r, k] = packed
                send(stag.at[p, r, k], rows.at[p, r, xs - k, 0], xs_sem.at[p, r, k], xr_sem.at[p, r, xs - k], x_dev(k))

    def forward_core(p, r):
        for k in range(1, xs):
            arrived(rows.at[p, r, k, 0], xs_sem.at[p, r, k], xr_sem.at[p, r, k], x_dev(k))
            send(rows.at[p, r, k, 0], rows.at[p, r, k, 1], cs_sem.at[p, r, k], cr_sem.at[p, r, k], c_dev)

    def feature(k, other):
        at = lax.rem(x + k, xs) * 2 + (1 - core if other else core)
        return pl.ds(pl.multiple_of(at * width, width), width)

    nt = (((1,), (1,)), ((), ()))

    def compute(p, r):
        first, second = None, None
        for k in range(xs):
            for o in range(2):
                if o == 1:
                    arrived(rows.at[p, r, k, 1], cs_sem.at[p, r, k], cr_sem.at[p, r, k], c_dev)
                piece = rows[p, r, k, o]
                if p == 0:
                    a = lax.dot_general(piece, wg[:, feature(k, o)], nt, preferred_element_type=F32)
                    b = lax.dot_general(piece, wu[:, feature(k, o)], nt, preferred_element_type=F32)
                    first = a if first is None else first + a
                    second = b if second is None else second + b
                else:
                    a = lax.dot_general(piece, wd[:, feature(k, o)], nt, preferred_element_type=F32)
                    first = a if first is None else first + a
        if p == 0:
            hidden = (jax.nn.silu(first) * second).astype(BF16)
        else:
            grad_gate = (first * fac[0, r]).astype(BF16)
            grad_up = (first * fac[1, r]).astype(BF16)
        for o in (1, 0):
            for k in range(xs):
                if p == 0:
                    res = jnp.dot(hidden, wd[:, feature(k, o)], preferred_element_type=F32)
                else:
                    res = jnp.dot(grad_gate, wg[:, feature(k, o)], preferred_element_type=F32)
                    res = res + jnp.dot(grad_up, wu[:, feature(k, o)], preferred_element_type=F32)
                if o == 1:
                    half_s[p, r, k] = res.astype(BF16)
                    send(half_s.at[p, r, k], half_r.at[p, r, k], hs_sem.at[p, r, k], hr_sem.at[p, r, k], c_dev)
                else:
                    keep[p, r, k] = res.astype(BF16)

    def join(p, r):
        for k in list(range(1, xs)) + [0]:
            arrived(half_r.at[p, r, k], hs_sem.at[p, r, k], hr_sem.at[p, r, k], c_dev)
            total = (keep[p, r, k].astype(F32) + half_r[p, r, k].astype(F32)).astype(BF16)
            if k == 0:
                mixin[p, r, 0] = total
            else:
                eo_s[p, r, k] = total
                send(eo_s.at[p, r, k], mixin.at[p, r, xs - k], es_sem.at[p, r, k], er_sem.at[p, r, xs - k], x_dev(k))

    def mix(p, r):
        for k in range(1, xs):
            arrived(mixin.at[p, r, k], es_sem.at[p, r, k], er_sem.at[p, r, k], x_dev(k))
        slot_ids = lax.broadcasted_iota(jnp.int32, (tokens, chunk), 1).astype(F32)
        pad = round_up(2 * xs, 8) - 2 * xs
        for c in (1, 0):
            lines = []
            for k in range(xs):
                at = lax.rem(x + k, xs)
                lines.append(meta_row(c, r, 2 * p * xs + at))
                lines.append(meta_row(c, r, (2 * p + 1) * xs + at))
            if pad:
                lines.append(jnp.zeros((pad, tokens), F32))
            cols = jnp.concatenate(lines, axis=0).T
            out = jnp.zeros((tokens, width), F32)
            for k in range(xs):
                mat = jnp.where(
                    slot_ids == cols[:, 2 * k : 2 * k + 1] + float(c * cap),
                    cols[:, 2 * k + 1 : 2 * k + 2], 0.0,
                ).astype(BF16)
                out = out + jnp.dot(mat, mixin[p, r, k], preferred_element_type=F32)
            if c == 1:
                yout[p, r] = out.astype(BF16)
                send(yout.at[p, r], yin.at[p, r], ry_sem.at[0, p, r], ry_sem.at[1, p, r], y_dev)
            else:
                zacc[p, r] = out

    def scatter_z(p, r):
        arrived(yin.at[p, r], ry_sem.at[0, p, r], ry_sem.at[1, p, r], y_dev)
        total = zacc[p, r] + yin[p, r].astype(F32)
        if r == 0:
            zacc[p, 0] = total
        else:
            zout[p, r] = total.astype(BF16)
            send(zout.at[p, r], zin.at[p, half - r], rzs_sem.at[p, r], rzr_sem.at[p, half - r], z_dev(r))

    def finish(p):
        total = zacc[p, 0]
        for r in range(1, half):
            arrived(zin.at[p, r], rzs_sem.at[p, r], rzr_sem.at[p, r], z_dev(r))
            total = total + zin[p, r].astype(F32)
        (fwd_out, bwd_out)[p][...] = total

    def factors(r):
        at = lax.broadcasted_iota(jnp.int32, (chunk, slots), 0)
        late = at >= cap
        turn = hi + r
        turn = jnp.where(turn >= half, turn - half, turn)
        origin = jnp.where(late, (turn * 2 + 1 - lo) * cap - cap, (turn * 2 + lo) * cap) + at
        hit = (origin == lax.broadcasted_iota(jnp.int32, (chunk, slots), 1)) & (at < 2 * cap)
        perm = jnp.where(hit, 1.0, 0.0).astype(BF16)
        gval = lax.dot_general(perm, sg[...], nt, preferred_element_type=F32)
        uval = lax.dot_general(perm, su[...], nt, preferred_element_type=F32)
        sig = jax.nn.sigmoid(gval)
        fac[0, r] = uval * sig * (1.0 + gval * (1.0 - sig))
        fac[1, r] = gval * sig

    back = list(range(half - 1, 0, -1))
    items = [(0, 0)] + [(0, r) for r in back] + [(1, r) for r in back] + [(1, 0)]
    count = len(items)
    stages = (
        (0, pack), (1, forward_core), (2, compute), (3, join), (4, mix), (5, scatter_z)
    )
    for load in loads[:2]:
        load.wait()
    for step in range(count + 5):
        if step + 1 < count:
            forward_y(*items[step + 1])
        if step == 2:
            for load in loads[2:]:
                load.wait()
        for lag, stage in stages:
            if 0 <= step - lag < count:
                stage(*items[step - lag])
        if step < half:
            factors(step)
    finish(0)
    finish(1)
    for copy in pending:
        copy.wait_send()


def body(
    fwd_resid, fwd_normed, fwd_routes, fwd_probs, bwd_grad, bwd_routes, bwd_probs,
    saved_gate, saved_up, w_gate, w_up, w_down,
):
    n = lax.axis_size("expert")
    dp = lax.axis_size("dp")
    sections = lax.axis_size("section")
    xs = dp // 2
    half = n // 2
    tokens, width = fwd_normed.shape[1:]
    top = fwd_routes.shape[2]
    slots, hidden = saved_gate.shape[2:]
    feats = w_gate.shape[2]
    cap = slots // n
    chunk = round_up(2 * cap, 8)
    meta_rows = 4 * xs
    vmem = pl.BlockSpec(memory_space=pltpu.VMEM)
    hbm = pl.BlockSpec(memory_space=pl.ANY)
    dma = pltpu.SemaphoreType.DMA
    out = jax.ShapeDtypeStruct((tokens, width), F32)
    fwd_sum, bwd_sum = pl.pallas_call(
        functools.partial(kernel, n, xs, top, cap),
        out_shape=(out, out),
        in_specs=[vmem] * 6 + [hbm] * 5,
        out_specs=(vmem, vmem),
        scratch_shapes=[
            pltpu.VMEM((hidden, slots), BF16),
            pltpu.VMEM((hidden, slots), BF16),
            pltpu.VMEM((hidden, feats), BF16),
            pltpu.VMEM((hidden, feats), BF16),
            pltpu.VMEM((hidden, feats), BF16),
            pltpu.VMEM((2, half, chunk, hidden), F32),
            pltpu.VMEM((n, meta_rows, tokens), F32),
            pltpu.VMEM((2, half, meta_rows, tokens), F32),
            pltpu.VMEM((half, meta_rows, tokens), F32),
            pltpu.VMEM((2, half, 2, tokens, width), BF16),
            pltpu.VMEM((2, half, xs, 2, chunk, width), BF16),
            pltpu.VMEM((2, half, xs, chunk, width), BF16),
            pltpu.VMEM((2, half, xs, chunk, width), BF16),
            pltpu.VMEM((2, half, xs, chunk, width), BF16),
            pltpu.VMEM((2, half, xs, chunk, width), BF16),
            pltpu.VMEM((2, half, xs, chunk, width), BF16),
            pltpu.VMEM((2, half, xs, chunk, width), BF16),
            pltpu.VMEM((2, half, tokens, width), BF16),
            pltpu.VMEM((2, half, tokens, width), BF16),
            pltpu.VMEM((2, half, tokens, width), F32),
            pltpu.VMEM((2, half, tokens, width), BF16),
            pltpu.VMEM((2, half, tokens, width), BF16),
            dma((5,)),
            dma((2, half)), dma((2, half)), dma((2, half)),
            dma((2, half)), dma((2, half)), dma((2, half)), dma((2, half)),
            dma((2, half, xs)), dma((2, half, xs)), dma((2, half, xs)), dma((2, half, xs)),
            dma((2, half, xs)), dma((2, half, xs)), dma((2, half, xs)), dma((2, half, xs)),
            dma((2, 2, half)), dma((2, half)), dma((2, half)),
        ],
        compiler_params=pltpu.CompilerParams(
            collective_id=0, has_side_effects=True, vmem_limit_bytes=60 * 1024 * 1024
        ),
    )(
        fwd_normed[0], bwd_grad[0],
        fwd_routes[0].T, fwd_probs[0].T, bwd_routes[0].T, bwd_probs[0].T,
        saved_gate[0, 0].T, saved_up[0, 0].T, w_gate[0, 0].T, w_up[0, 0].T, w_down[0, 0],
    )
    fwd_next = (fwd_resid.astype(F32) + fwd_sum[None]).astype(BF16)
    bwd_next = bwd_sum[None].astype(BF16)
    if sections > 1:
        up = [(i, (i + 1) % sections) for i in range(sections)]
        fwd_next = lax.ppermute(fwd_next, "section", up)
        bwd_next = lax.ppermute(bwd_next, "section", [(j, i) for i, j in up])
    return (fwd_next, bwd_next)


def solution(mesh):
    tok = P("section", "expert", "dp")
    route = P("section", "expert", None)
    unit = P("section", ("expert", "dp"), None, None)
    return jax.shard_map(
        body,
        mesh=mesh,
        in_specs=(tok, tok, route, route, tok, route, route, unit, unit, unit, unit, unit),
        out_specs=(tok, tok),
        check_vma=False,
    )
```

time: 108 us -> 89.5 us (0.83)
  Pallas kernels: 96.4 us -> 86.3 us
  local copies, waits for them, and re-layouts: 8.42 us -> 0.01 us
    pallas_call x1, Pallas kernels: 96.4 us -> 86.3 us  [body(): pl.pallas_call(functools.partial(kernel, n, xs, top, cap), out_shape=(out...]
    unnamed x12 -> x4, local copies, waits for them, and re-layouts: 8.42 us -> 0.01 us
    convert_element_type x0 -> x2, other arithmetic: none -> 2.35 us  [the longest x1 1.67 us: body(): fwd_next = (fwd_resid.astype(F32) + fwd_sum[None]).astype(BF16)]
    concatenate x1 -> x0, other arithmetic: 1.31 us -> none  [body(): jnp.concatenate([fwd_routes[0].astype(F32).T, fwd_probs[0].T, bwd_routes[...]
where the time goes in v1:
time: 89.5 us; the launch traced here: 89.4 us
  Pallas kernels  86.3 us (96%)
  other arithmetic  2.35 us (3%)
    pallas_call x1, Pallas kernels, body(): pl.pallas_call(functools.partial(kernel, n, xs, top, cap), out_shape=(out...  86.3 us

profile of v1, /device:TPU:0, one launch (start us, length us, event | category | flops | bytes accessed | tf_op | source)
XLA Modules:
  0.0 89.4 jit_solution(837061336348470368)
XLA Ops:
  0.6 0.0 copy-start.1
  0.6 86.3 %shard_map.131 = (f32[128,512]{1,0:T(8,128)}, f32[128,512]{1,0:T(8,128)}) custom-call(bf16[128,512]{1,0:T(8,128)(2,1)} %bitcast.38, bf16[128,512]{1,0:T(8,128)(2,1)} %bitcast.39, s32[8,128]{1,0:T(8,128)} %bitcast.40, f32[8,128]{1,0:T(8,128)} %bitcast.41, s32[8,128]{1,0:T(8,128)} %bitcast.42, f32[8,128]{1,0:T(8,128)} %bitcast.43, bf16[192,520]{1,0:T(8,128)(2,1)} %bitcast.36, ...), custom_call_target="tpu_custom_call" | custom-call | tf_op jit(solution)/shard_map/pallas_call | solution.py:316
  87.0 0.0 copy-done.1
  87.0 0.0 copy-start
  87.0 1.7 %fusion = bf16[1,128,512]{2,1,0:T(8,128)(2,1)} fusion(f32[128,512]{1,0:T(8,128)} %get-tuple-element.4, bf16[1,128,512]{2,1,0:T(8,128)(2,1)S(1)} %copy-done.1), kind=kLoop, calls=%fused_computation.1 | loop fusion | flops 196608 | bytes 524288 | tf_op jit(solution)/shard_map/convert_element_type | solution.py:359
  88.7 0.0 copy-done
  88.7 0.7 convert_bitcast_fusion
Async XLA Ops:
  0.6 86.4 %copy-start.1 = (bf16[1,128,512]{2,1,0:T(8,128)(2,1)S(1)}, bf16[1,128,512]{2,1,0:T(8,128)(2,1)}, u32[]{:S(2)}) copy-start(bf16[1,128,512]{2,1,0:T(8,128)(2,1)} %param.12) | copy-start | bytes 393220
  87.0 1.7 %copy-start = (f32[128,512]{1,0:T(8,128)S(1)}, f32[128,512]{1,0:T(8,128)}, u32[]{:S(2)}) copy-start(f32[128,512]{1,0:T(8,128)} %get-tuple-element.5) | copy-start | bytes 786436

commit v2 on v1

--- a/solution.py
+++ b/solution.py
@@ -269,23 +269,19 @@
         fac[1, r] = gval * sig
 
     back = list(range(half - 1, 0, -1))
-    items = [(0, 0)] + [(0, r) for r in back] + [(1, r) for r in back] + [(1, 0)]
+    items = [(0, 0), (1, 0)] + [(0, r) for r in back] + [(1, r) for r in back]
     count = len(items)
-    stages = (
-        (0, pack), (1, forward_core), (2, compute), (3, join), (4, mix), (5, scatter_z)
-    )
+    stages = ((0, pack), (-1, forward_y), (1, forward_core), (1, compute), (2, mix), (1, join), (3, scatter_z))
     for load in loads[:2]:
         load.wait()
-    for step in range(count + 5):
-        if step + 1 < count:
-            forward_y(*items[step + 1])
-        if step == 2:
+    for step in range(-2, count + 9):
+        if step == 1:
             for load in loads[2:]:
                 load.wait()
         for lag, stage in stages:
             if 0 <= step - lag < count:
                 stage(*items[step - lag])
-        if step < half:
+        if 0 <= step < half:
             factors(step)
     finish(0)
     finish(1)

time: 89.5 us -> 85.8 us (0.959)
  Pallas kernels: 86.3 us -> 82.6 us
    pallas_call x1, Pallas kernels: 86.3 us -> 82.6 us  [body(): pl.pallas_call(functools.partial(kernel, n, xs, top, cap), out_shape=(out...]
where the time goes in v2:
time: 85.8 us; the launch traced here: 85.7 us
  Pallas kernels  82.6 us (96%)
  other arithmetic  2.35 us (3%)
    pallas_call x1, Pallas kernels, body(): pl.pallas_call(functools.partial(kernel, n, xs, top, cap), out_shape=(out...  82.6 us

profile of v2, /device:TPU:0, one launch (start us, length us, event | category | flops | bytes accessed | tf_op | source)
XLA Modules:
  0.0 85.7 jit_solution(16621018655477188216)
XLA Ops:
  0.6 0.0 copy-start.1
  0.6 82.6 %shard_map.131 = (f32[128,512]{1,0:T(8,128)}, f32[128,512]{1,0:T(8,128)}) custom-call(bf16[128,512]{1,0:T(8,128)(2,1)} %bitcast.38, bf16[128,512]{1,0:T(8,128)(2,1)} %bitcast.39, s32[8,128]{1,0:T(8,128)} %bitcast.40, f32[8,128]{1,0:T(8,128)} %bitcast.41, s32[8,128]{1,0:T(8,128)} %bitcast.42, f32[8,128]{1,0:T(8,128)} %bitcast.43, bf16[192,520]{1,0:T(8,128)(2,1)} %bitcast.36, ...), custom_call_target="tpu_custom_call" | custom-call | tf_op jit(solution)/shard_map/pallas_call | solution.py:312
  83.3 0.0 copy-done.1
  83.3 0.0 copy-start
  83.3 1.7 %fusion = bf16[1,128,512]{2,1,0:T(8,128)(2,1)} fusion(f32[128,512]{1,0:T(8,128)} %get-tuple-element.4, bf16[1,128,512]{2,1,0:T(8,128)(2,1)S(1)} %copy-done.1), kind=kLoop, calls=%fused_computation.1 | loop fusion | flops 196608 | bytes 524288 | tf_op jit(solution)/shard_map/convert_element_type | solution.py:355
  85.0 0.0 copy-done
  85.0 0.7 convert_bitcast_fusion
Async XLA Ops:
  0.6 82.7 %copy-start.1 = (bf16[1,128,512]{2,1,0:T(8,128)(2,1)S(1)}, bf16[1,128,512]{2,1,0:T(8,128)(2,1)}, u32[]{:S(2)}) copy-start(bf16[1,128,512]{2,1,0:T(8,128)(2,1)} %param.12) | copy-start | bytes 393220
  83.3 1.7 %copy-start = (f32[128,512]{1,0:T(8,128)S(1)}, f32[128,512]{1,0:T(8,128)}, u32[]{:S(2)}) copy-start(f32[128,512]{1,0:T(8,128)} %get-tuple-element.5) | copy-start | bytes 786436
